TPU v7x, 32 devices: a whole 2x2x4 slice. The times are simulated.
32 devices in a mesh: fsdp: 8 (over z, x), rep: 4 (over y, core).
Axes of the slice: x: 2, y: 2, z: 4, core: 2. Of those that a mesh axis runs over, the one named last changes fastest.
Arguments:
- tokens_x: bfloat16 [4096, 8192], P(('fsdp', 'rep')), may hold values from -6 to 6
- cotangent: bfloat16 [4096, 128], P(('fsdp', 'rep')), may hold values from -1 to 1
- master_weight: float32 [8192, 128], P('fsdp'), may hold values from -0.015625 to 0.015625
- first_moment: float32 [8192, 128], P('fsdp'), may hold values from -6 to 6
- second_moment: float32 [8192, 128], P('fsdp'), may hold values from 0.5 to 2
- hidden_dec: bfloat16 [2, 64, 8192], P(None, ('fsdp', 'rep')), may hold values from -6 to 6
- queries: bfloat16 [2, 64, 1024], P(None, ('fsdp', 'rep')), may hold values from -64 to 64
- new_values: bfloat16 [2, 64, 128], P(None, ('fsdp', 'rep')), may hold values from -6 to 6
- key_cache: bfloat16 [64, 1024, 128], P(('fsdp', 'rep')), may hold values from -64 to 64
- value_cache: bfloat16 [64, 1024, 128], P(('fsdp', 'rep')), may hold values from -6 to 6
- cache_lengths: int32 [64], P(('fsdp', 'rep')), may hold values from 2 to 1022, as said below
Outputs:
- weight_next: float32 [8192, 128], P('fsdp')
- first_next: float32 [8192, 128], P('fsdp')
- second_next: float32 [8192, 128], P('fsdp')
- rollout_weight: bfloat16 [8192, 128], replicated
- fresh_keys: bfloat16 [2, 64, 128], P(None, ('fsdp', 'rep'))
- attended: bfloat16 [2, 64, 1024], P(None, ('fsdp', 'rep'))
Inputs may be any that keep to these rules, and one draw needn't show every extreme that they name: `cache_lengths`: some row has exactly 1022 filled slots.
All inputs are finite; a program needn't handle non-finite values. Where the computation divides by a largest or mean magnitude, that divisor is 1e-20 or more.
Results may differ from a plain program's by a relative error of at most 0.0049.
Values may be sent and summed in bfloat16 or wider, within the bound.
A program may use at most 64 MiB of HBM per device.

v0:
```python
import math
import jax
import jax.numpy as jnp
from jax import lax
from jax.sharding import PartitionSpec as P

D = 8192
BLOCK = 128
beta_one = 0.9
beta_two = 0.95
adam_eps = 1e-08
learn_rate = 0.0003
weight_decay = 0.1
step_count = 100
rope_theta = 1000000.0
peak_eps = 1e-06


def adamw(weight, first, second, gradient):
    first_new = beta_one * first + (1.0 - beta_one) * gradient
    second_new = beta_two * second + (1.0 - beta_two) * gradient * gradient
    first_hat = first_new / (1.0 - beta_one**step_count)
    second_hat = second_new / (1.0 - beta_two**step_count)
    weight_new = weight - learn_rate * (
        first_hat / (jnp.sqrt(second_hat) + adam_eps) + weight_decay * weight
    )
    return (weight_new, first_new, second_new)


def rotate(values, positions):
    half = values.shape[-1] // 2
    freq = rope_theta ** (-jnp.arange(half, dtype=jnp.float32) * 2.0 / values.shape[-1])
    angle = positions.astype(jnp.float32)[..., None] * freq
    cosine = jnp.cos(angle)
    sine = jnp.sin(angle)
    first_half = values[..., :half]
    second_half = values[..., half:]
    return jnp.concatenate(
        [first_half * cosine - second_half * sine, second_half * cosine + first_half * sine],
        axis=-1,
    )


def project_keys(hidden_size, quantized_weight, scales, lengths):
    decode_step_count, row_count, block_width = hidden_size.shape
    block_count = scales.shape[0]
    part_count = jnp.einsum(
        "qht,hti->qhi",
        hidden_size.reshape(decode_step_count * row_count, block_count, block_width // block_count),
        quantized_weight.reshape(block_count, block_width // block_count, -1),
        preferred_element_type=jnp.float32,
    )
    raw = jnp.sum(part_count * scales[None, :, None], axis=1).reshape(
        decode_step_count, row_count, -1
    )
    positions = lengths[None, :] + jnp.arange(decode_step_count, dtype=jnp.int32)[:, None]
    return rotate(raw, positions).astype(jnp.bfloat16)


def attend(query, cache_keys, cache_values, fresh, fresh_values, lengths):
    decode_step_count, row_count, joined = query.shape
    head_dim = cache_keys.shape[-1]
    heads = joined // head_dim
    valid = jnp.arange(cache_keys.shape[1], dtype=jnp.int32)[None, None, :] < lengths[:, None, None]
    outputs = []
    for section_index in range(decode_step_count):
        query_now = query[section_index].reshape(row_count, heads, head_dim)
        scores_c = jnp.einsum(
            "rhd,rcd->rhc", query_now, cache_keys, preferred_element_type=jnp.float32
        ) / math.sqrt(head_dim)
        scores_f = jnp.einsum(
            "rhd,trd->rht", query_now, fresh, preferred_element_type=jnp.float32
        ) / math.sqrt(head_dim)
        scores_c = jnp.where(valid, scores_c, -jnp.inf)
        scores_f = jnp.where(
            (jnp.arange(decode_step_count) <= section_index)[None, None, :], scores_f, -jnp.inf
        )
        peak = jnp.maximum(jnp.max(scores_c, axis=2), jnp.max(scores_f, axis=2))[:, :, None]
        exp_c = jnp.exp(scores_c - peak)
        exp_f = jnp.exp(scores_f - peak)
        total = jnp.sum(exp_c, axis=2, keepdims=True) + jnp.sum(exp_f, axis=2, keepdims=True)
        prob_c = (exp_c / total).astype(jnp.bfloat16)
        prob_f = (exp_f / total).astype(jnp.bfloat16)
        mixed = jnp.einsum("rhc,rcd->rhd", prob_c, cache_values, preferred_element_type=jnp.float32)
        mixed = mixed + jnp.einsum(
            "rht,trd->rhd", prob_f, fresh_values, preferred_element_type=jnp.float32
        )
        outputs.append(mixed.reshape(row_count, joined).astype(jnp.bfloat16))
    return jnp.stack(outputs)


def shards(
    tokens_x,
    cotangent,
    master_weight,
    first_moment,
    second_moment,
    hidden_dec,
    queries,
    new_values,
    key_cache,
    value_cache,
    cache_lengths,
):
    shard_rows = master_weight.shape[0]
    partial_grad = lax.psum_scatter(
        lax.dot_general(
            tokens_x, cotangent, (((0,), (0,)), ((), ())), preferred_element_type=jnp.float32
        ),
        "fsdp",
        scatter_dimension=0,
        tiled=True,
    )
    gradient = lax.psum(partial_grad, "rep")
    weight_next, first_next, second_next = adamw(
        master_weight, first_moment, second_moment, gradient
    )
    block_count = D // BLOCK
    row_ids = lax.axis_index("fsdp") * shard_rows + jnp.arange(shard_rows, dtype=jnp.int32)
    member = (row_ids // BLOCK)[:, None] == jnp.arange(block_count, dtype=jnp.int32)[None, :]
    row_peak = jnp.max(jnp.abs(weight_next), axis=1)
    local_peaks = jnp.max(jnp.where(member, row_peak[:, None], 0.0), axis=0)
    scales = lax.pmax(local_peaks, "fsdp") + peak_eps
    row_scale = jnp.sum(jnp.where(member, scales[None, :], 0.0), axis=1)
    local_quant = (weight_next / row_scale[:, None]).astype(jnp.bfloat16)
    rollout_weight = lax.all_gather(local_quant, "fsdp", axis=0, tiled=True)
    fresh_keys = project_keys(hidden_dec, rollout_weight, scales, cache_lengths)
    attended = attend(queries, key_cache, value_cache, fresh_keys, new_values, cache_lengths)
    return (weight_next, first_next, second_next, rollout_weight, fresh_keys, attended)


def solution(mesh):
    return jax.shard_map(
        shards,
        mesh=mesh,
        in_specs=(
            P(("fsdp", "rep"), None),
            P(("fsdp", "rep"), None),
            P("fsdp", None),
            P("fsdp", None),
            P("fsdp", None),
            P(None, ("fsdp", "rep"), None),
            P(None, ("fsdp", "rep"), None),
            P(None, ("fsdp", "rep"), None),
            P(("fsdp", "rep"), None, None),
            P(("fsdp", "rep"), None, None),
            P(("fsdp", "rep")),
        ),
        out_specs=(
            P("fsdp", None),
            P("fsdp", None),
            P("fsdp", None),
            P(),
            P(None, ("fsdp", "rep"), None),
            P(None, ("fsdp", "rep"), None),
        ),
        check_vma=False,
    )
```

profile of v0, /device:TPU:0, one launch (start us, length us, event | category | flops | bytes accessed | tf_op | source)
XLA Modules:
  0.0 224.9 jit_solution(2394929650028422589)
XLA Ops:
  7.2 0.0 copy-start
  7.2 0.0 reduce-scatter.2.cloned.1.call-start
  7.2 1.5 copy-done
  8.8 3.4 %fusion.52 = f32[8192,128]{1,0:T(8,128)} fusion(bf16[128,8192]{1,0:T(8,128)(2,1)S(1)} %copy-done, bf16[128,128]{1,0:T(8,128)(2,1)} %param.12), kind=kOutput, calls=%fused_computation.92 | convolution fusion | flops 268435456 | bytes 6324224 | tf_op jit(solution)/shard_map/dot_general | solution.py:107
  12.2 0.0 reduce-scatter.2.cloned.1.call-update
  12.2 0.0 all-reduce.2.cloned.1.call-start
  12.3 91.1 %reduce-scatter.2.cloned.1.call-done = f32[1024,128]{1,0:T(8,128)} async-done(((f32[8192,128]{1,0:T(8,128)}), f32[1024,128]{1,0:T(8,128)}) %reduce-scatter.2.cloned.1.call-update) | async-done | bytes 524304 | tf_op jit(solution)/shard_map/reduce_scatter | solution.py:106
  103.4 0.0 all-reduce.2.cloned.1.call-update
  103.4 0.0 all-gather.2.cloned.1.call-start
  103.5 0.0 copy-start.4
  103.5 0.0 copy-start.6
  103.5 0.0 copy-start.5
  103.5 0.0 copy-start.1
  103.6 35.3 %all-reduce.2.cloned.1.call-done = f32[1024,128]{1,0:T(8,128)} async-done(((f32[1024,128]{1,0:T(8,128)}), f32[1024,128]{1,0:T(8,128)}) %all-reduce.2.cloned.1.call-update) | async-done | bytes 524304 | tf_op jit(solution)/shard_map/psum | solution.py:114
  138.8 2.9 %abs_reduce_fusion = (f32[1024]{0:T(1024)S(1)}, f32[1024,128]{1,0:T(8,128)S(1)}, f32[1024,128]{1,0:T(8,128)}, f32[1024,128]{1,0:T(8,128)}) fusion(f32[1024,128]{1,0:T(8,128)} %param.13, f32[1024,128]{1,0:T(8,128)} %all-reduce.2.cloned.1.call-done, f32[1024,128]{1,0:T(8,128)} %param.14, f32[1024,128]{1,0:T(8,128)} %param.15), kind=kLoop, calls=%fused_computation.19 | loop fusion | flops 2227200 | bytes 3674112 | tf_op jit(solution)/shard_map/reduce_max | solution.py:121
  141.7 0.1 select_reduce_fusion.1
  141.9 21.3 %pmax.7 = f32[64]{0:T(128)S(1)} all-reduce(f32[64]{0:T(128)S(1)} %select_reduce_fusion.1), channel_id=1, replica_groups=mesh['fsdp'=8,'rep'=4] {'fsdp'}, use_global_device_ids=true, to_apply=%region_4.5 | all-reduce | flops 64 | bytes 512 | tf_op jit(solution)/shard_map/pmax | solution.py:123
  163.2 0.1 select_reduce_fusion
  163.3 0.0 copy-done.3
  163.3 0.9 divide_convert_fusion
  164.3 0.0 all-gather.2.cloned.1.call-update
  164.3 0.0 copy-done.4
  164.3 0.1 reshape.145
  164.4 0.0 copy-done.6
  164.4 0.1 add_convert_fusion
  164.5 0.1 iota_compare_fusion.1
  164.6 0.0 copy-done.5
  164.6 0.0 copy-start.7
  164.6 0.3 fusion.50
  164.9 0.3 fusion.48
  165.3 44.7 %all-gather.2.cloned.1.call-done = bf16[8192,128]{1,0:T(8,128)(2,1)} async-done(((bf16[1024,128]{1,0:T(8,128)(2,1)}), bf16[8192,128]{1,0:T(8,128)(2,1)}) %all-gather.2.cloned.1.call-update) | async-done | bytes 2097168 | tf_op jit(solution)/shard_map/all_gather | solution.py:126
  210.0 2.2 fusion
  212.2 0.1 fusion.47
  212.3 0.1 fusion.37
  212.4 0.1 pad_maximum_fusion.1
  212.5 0.6 copy.32
  213.1 0.1 fusion.49
  213.2 0.1 fusion.51
  213.4 0.2 fusion.12
  213.5 0.0 copy-done.2
  213.5 0.2 fusion.14
  213.8 0.0 copy-done.7
  213.8 0.2 fusion.4
  214.0 0.2 fusion.11
  214.2 0.2 fusion.13
  214.5 0.2 fusion.3
  214.7 0.6 pad_maximum_fusion
  215.3 3.0 %copy.73 = bf16[8192,128]{1,0:T(8,128)(2,1)} copy(bf16[8192,128]{1,0:T(8,128)(2,1)} %all-gather.2.cloned.1.call-done) | data formatting | bytes 4194304
  (17 shorter events, 0.2 us)
Async XLA Ops:
  7.2 1.6 copy-start
  7.2 96.2 %reduce-scatter.2.cloned.1.call-start = ((), (), s32[]{:S(2)}) async-start(), calls=%async_computation.1 | async-start | bytes 4718592 | tf_op jit(solution)/shard_map/reduce_scatter | solution.py:106
  12.2 126.6 %all-reduce.2.cloned.1.call-start = ((), (), s32[]{:S(2)}) async-start(), calls=%async_computation.2 | async-start | bytes 1048576 | tf_op jit(solution)/shard_map/psum | solution.py:114
  103.4 106.5 %all-gather.2.cloned.1.call-start = ((), (), s32[]{:S(2)}) async-start(), calls=%async_computation.3 | async-start | bytes 2359296 | tf_op jit(solution)/shard_map/all_gather | solution.py:126
  103.5 60.8 %copy-start.4 = (bf16[2,2,8192]{2,1,0:T(2,128)(2,1)S(1)}, bf16[2,2,8192]{2,1,0:T(2,128)(2,1)}, u32[]{:S(2)}) copy-start(bf16[2,2,8192]{2,1,0:T(2,128)(2,1)} %param.16) | copy-start | bytes 196612
  103.5 60.9 %copy-start.6 = (s32[2]{0:T(128)S(1)}, s32[2]{0:T(128)}, u32[]{:S(2)}) copy-start(s32[2]{0:T(128)} %param.21) | copy-start | bytes 28
  103.5 61.0 %copy-start.5 = (bf16[2,2,1024]{2,1,0:T(2,128)(2,1)S(1)}, bf16[2,2,1024]{2,1,0:T(2,128)(2,1)}, u32[]{:S(2)}) copy-start(bf16[2,2,1024]{2,1,0:T(2,128)(2,1)} %param.17) | copy-start | bytes 24580
  103.5 61.0 %copy-start.1 = (bf16[2,1024,128]{2,1,0:T(8,128)(2,1)S(1)}, bf16[2,1024,128]{2,1,0:T(8,128)(2,1)}, u32[]{:S(2)}) copy-start(bf16[2,1024,128]{2,1,0:T(8,128)(2,1)} %param.19) | copy-start | bytes 1572868
  141.7 21.6 %copy-start.3 = (f32[1024,128]{1,0:T(8,128)}, f32[1024,128]{1,0:T(8,128)S(1)}, u32[]{:S(2)}) copy-start(f32[1024,128]{1,0:T(8,128)S(1)} %get-tuple-element.48) | copy-start | bytes 1572868
  164.3 49.3 %copy-start.2 = (bf16[2,1024,128]{2,1,0:T(8,128)(2,1)S(1)}, bf16[2,1024,128]{2,1,0:T(8,128)(2,1)}, u32[]{:S(2)}) copy-start(bf16[2,1024,128]{2,1,0:T(8,128)(2,1)} %param.20) | copy-start | bytes 1572868
  164.6 49.2 %copy-start.7 = (bf16[2,2,128]{2,1,0:T(2,128)(2,1)S(1)}, bf16[2,2,128]{2,1,0:T(2,128)(2,1)}, u32[]{:S(2)}) copy-start(bf16[2,2,128]{2,1,0:T(2,128)(2,1)} %param.18) | copy-start | bytes 3076
Sparse Core Ops, SparseCore 0:
  12.3 91.0 reduce-scatter.1
  105.8 33.0 all-reduce.1
  164.4 45.5 all-gather.1
where the time goes:
time: 225 us
  waiting for transfers between devices  171 us (76%)
  blocking collectives  21.3 us (9%)
  between operations  13.9 us (6%)
  matrix products  7.48 us (3%)
  other arithmetic  5.48 us (2%)
  local copies, waits for them, and re-layouts  5.36 us (2%)
    reduce_scatter x1, waiting for transfers between devices, shards(): lax.psum_scatter(lax.dot_general(tokens_x, cotangent, (((0,), (0,)), ((),...  91.1 us
    all_gather x1, waiting for transfers between devices, shards(): rollout_weight = lax.all_gather(local_quant, 'fsdp', axis=0, tiled=True)  44.7 us
    psum x1, waiting for transfers between devices, shards(): gradient = lax.psum(partial_grad, 'rep')  35.3 us
    pmax x1, blocking collectives, shards(): scales = lax.pmax(local_peaks, 'fsdp') + peak_eps  21.3 us
    unnamed x19, local copies, waits for them, and re-layouts  5.2 us
  transfers between devices with their start and end apart: 3, of which 3 were waited for; matrix products, arithmetic and copies ran while one was open for 0% of the time, Pallas kernels for 0%

commit v1 on v0

--- a/solution.py
+++ b/solution.py
@@ -111,7 +111,7 @@
         scatter_dimension=0,
         tiled=True,
     )
-    gradient = lax.psum(partial_grad, "rep")
+    gradient = jnp.sum(lax.all_gather(partial_grad, "rep"), axis=0)
     weight_next, first_next, second_next = adamw(
         master_weight, first_moment, second_moment, gradient
     )

time: 225 us -> 216 us (0.960)
  waiting for transfers between devices: 171 us -> 159 us
  other arithmetic: 5.48 us -> 8.09 us
    psum x1 -> x0, waiting for transfers between devices: 35.3 us -> none  [shards(): gradient = lax.psum(partial_grad, 'rep')]
    all_gather x0 -> x1, waiting for transfers between devices: none -> 23.7 us  [shards(): gradient = jnp.sum(lax.all_gather(partial_grad, 'rep'), axis=0)]
    reduce_sum x0 -> x1, other arithmetic: none -> 2.55 us  [shards(): gradient = jnp.sum(lax.all_gather(partial_grad, 'rep'), axis=0)]
where the time goes in v1:
time: 216 us
  waiting for transfers between devices  159 us (74%)
  blocking collectives  21.3 us (10%)
  between operations  13.9 us (6%)
  other arithmetic  8.09 us (4%)
  matrix products  7.48 us (3%)
  local copies, waits for them, and re-layouts  5.35 us (2%)
    reduce_scatter x1, waiting for transfers between devices, shards(): lax.psum_scatter(lax.dot_general(tokens_x, cotangent, (((0,), (0,)), ((),...  91.1 us
    all_gather x1, waiting for transfers between devices, shards(): rollout_weight = lax.all_gather(local_quant, 'fsdp', axis=0, tiled=True)  44.6 us
    all_gather x1, waiting for transfers between devices, shards(): gradient = jnp.sum(lax.all_gather(partial_grad, 'rep'), axis=0)  23.7 us
    pmax x1, blocking collectives, shards(): scales = lax.pmax(local_peaks, 'fsdp') + peak_eps  21.3 us
    unnamed x19, local copies, waits for them, and re-layouts  5.19 us
  transfers between devices with their start and end apart: 3, of which 3 were waited for; matrix products, arithmetic and copies ran while one was open for 0% of the time, Pallas kernels for 0%

profile of v1, /device:TPU:0, one launch (start us, length us, event | category | flops | bytes accessed | tf_op | source)
XLA Modules:
  0.0 215.7 jit_solution(10120802812732415479)
XLA Ops:
  7.2 0.0 copy-start
  7.2 0.0 reduce-scatter.2.cloned.1.call-start
  7.2 1.5 copy-done
  8.8 3.4 %fusion.52 = f32[8192,128]{1,0:T(8,128)} fusion(bf16[128,8192]{1,0:T(8,128)(2,1)S(1)} %copy-done, bf16[128,128]{1,0:T(8,128)(2,1)} %param.12), kind=kOutput, calls=%fused_computation.92 | convolution fusion | flops 268435456 | bytes 6324224 | tf_op jit(solution)/shard_map/dot_general | solution.py:107
  12.2 0.0 reduce-scatter.2.cloned.1.call-update
  12.2 0.0 all-gather.6.cloned.1.call-start
  12.3 91.1 %reduce-scatter.2.cloned.1.call-done = f32[1024,128]{1,0:T(8,128)} async-done(((f32[8192,128]{1,0:T(8,128)}), f32[1024,128]{1,0:T(8,128)}) %reduce-scatter.2.cloned.1.call-update) | async-done | bytes 524304 | tf_op jit(solution)/shard_map/reduce_scatter | solution.py:106
  103.4 0.0 all-gather.6.cloned.1.call-update
  103.4 0.0 all-gather.4.cloned.1.call-start
  103.5 23.7 %all-gather.6.cloned.1.call-done = f32[4096,128]{1,0:T(8,128)} async-done(((f32[1024,128]{1,0:T(8,128)}), f32[4096,128]{1,0:T(8,128)}) %all-gather.6.cloned.1.call-update) | async-done | bytes 2097168 | tf_op jit(solution)/shard_map/all_gather | solution.py:114
  127.2 2.5 %reduce_sum.65 = f32[1024,128]{1,0:T(8,128)} reduce(f32[4,1024,128]{2,1,0:T(8,128)} %bitcast.43, f32[]{:T(128)} %constant.23.clone.1), dimensions={0}, to_apply=%region_1.0 | reduce | flops 393216 | bytes 2621444 | tf_op jit(solution)/shard_map/reduce_sum | solution.py:114
  129.7 0.0 copy-start.4
  129.7 0.0 copy-start.6
  129.7 3.0 %abs_reduce_fusion = (f32[1024]{0:T(1024)S(1)}, f32[1024,128]{1,0:T(8,128)S(1)}, f32[1024,128]{1,0:T(8,128)}, f32[1024,128]{1,0:T(8,128)}) fusion(f32[1024,128]{1,0:T(8,128)} %param.13, f32[1024,128]{1,0:T(8,128)} %reduce_sum.65, f32[1024,128]{1,0:T(8,128)} %param.14, f32[1024,128]{1,0:T(8,128)} %param.15), kind=kLoop, calls=%fused_computation.19 | loop fusion | flops 2227200 | bytes 3674112 | tf_op jit(solution)/shard_map/reduce_max | solution.py:121
  132.7 0.1 select_reduce_fusion.1
  132.8 21.3 %pmax.7 = f32[64]{0:T(128)S(1)} all-reduce(f32[64]{0:T(128)S(1)} %select_reduce_fusion.1), channel_id=1, replica_groups=mesh['fsdp'=8,'rep'=4] {'fsdp'}, use_global_device_ids=true, to_apply=%region_4.5 | all-reduce | flops 64 | bytes 512 | tf_op jit(solution)/shard_map/pmax | solution.py:123
  154.2 0.1 select_reduce_fusion
  154.3 0.0 copy-done.3
  154.3 0.9 divide_convert_fusion
  155.2 0.0 all-gather.4.cloned.1.call-update
  155.3 0.0 copy-done.4
  155.3 0.1 reshape.145
  155.4 0.0 copy-done.6
  155.4 0.1 add_convert_fusion
  155.4 0.1 iota_compare_fusion.1
  155.5 0.0 copy-done.5
  155.5 0.0 copy-done.1
  155.5 0.0 copy-start.7
  155.6 0.3 fusion.50
  155.9 0.3 fusion.48
  156.2 44.6 %all-gather.4.cloned.1.call-done = bf16[8192,128]{1,0:T(8,128)(2,1)} async-done(((bf16[1024,128]{1,0:T(8,128)(2,1)}), bf16[8192,128]{1,0:T(8,128)(2,1)}) %all-gather.4.cloned.1.call-update) | async-done | bytes 2097168 | tf_op jit(solution)/shard_map/all_gather | solution.py:126
  200.8 2.2 %fusion = f32[128,4]{0,1:T(4,128)S(1)} fusion(bf16[64,128,128]{2,1,0:T(8,128)(2,1)} %bitcast.42, bf16[4,64,128]{2,1,0:T(8,128)(2,1)S(1)} %reshape.145, f32[64]{0:T(128)S(1)} %broadcast_add_fusion), kind=kOutput, calls=%fused_computation.1 | convolution fusion | flops 8453632 | bytes 2164992 | tf_op jit(solution)/shard_map/qht,hti->qhi/dot_general | solution.py:47
  203.1 0.1 fusion.47
  203.1 0.1 fusion.37
  203.3 0.1 pad_maximum_fusion.1
  203.4 0.6 copy.32
  203.9 0.1 fusion.49
  204.1 0.1 fusion.51
  204.2 0.2 fusion.12
  204.4 0.0 copy-done.2
  204.4 0.2 fusion.14
  204.6 0.0 copy-done.7
  204.6 0.2 fusion.4
  204.9 0.2 fusion.11
  205.1 0.2 fusion.13
  205.3 0.2 fusion.3
  205.5 0.6 pad_maximum_fusion
  206.2 3.0 %copy.72 = bf16[8192,128]{1,0:T(8,128)(2,1)} copy(bf16[8192,128]{1,0:T(8,128)(2,1)} %all-gather.4.cloned.1.call-done) | data formatting | bytes 4194304
  (18 shorter events, 0.2 us)
Async XLA Ops:
  7.2 1.6 copy-start
  7.2 96.2 %reduce-scatter.2.cloned.1.call-start = ((), (), s32[]{:S(2)}) async-start(), calls=%async_computation.1 | async-start | bytes 4718592 | tf_op jit(solution)/shard_map/reduce_scatter | solution.py:106
  12.2 115.0 %all-gather.6.cloned.1.call-start = ((), (), s32[]{:S(2)}) async-start(), calls=%async_computation.3 | async-start | bytes 2621440 | tf_op jit(solution)/shard_map/all_gather | solution.py:114
  103.4 97.4 %all-gather.4.cloned.1.call-start = ((), (), s32[]{:S(2)}) async-start(), calls=%async_computation.2 | async-start | bytes 2359296 | tf_op jit(solution)/shard_map/all_gather | solution.py:126
  129.7 25.5 %copy-start.4 = (bf16[2,2,8192]{2,1,0:T(2,128)(2,1)S(1)}, bf16[2,2,8192]{2,1,0:T(2,128)(2,1)}, u32[]{:S(2)}) copy-start(bf16[2,2,8192]{2,1,0:T(2,128)(2,1)} %param.16) | copy-start | bytes 196612
  129.7 25.6 %copy-start.6 = (s32[2]{0:T(128)S(1)}, s32[2]{0:T(128)}, u32[]{:S(2)}) copy-start(s32[2]{0:T(128)} %param.21) | copy-start | bytes 28
  129.7 25.8 %copy-start.5 = (bf16[2,2,1024]{2,1,0:T(2,128)(2,1)S(1)}, bf16[2,2,1024]{2,1,0:T(2,128)(2,1)}, u32[]{:S(2)}) copy-start(bf16[2,2,1024]{2,1,0:T(2,128)(2,1)} %param.17) | copy-start | bytes 24580
  129.7 25.8 %copy-start.1 = (bf16[2,1024,128]{2,1,0:T(8,128)(2,1)S(1)}, bf16[2,1024,128]{2,1,0:T(8,128)(2,1)}, u32[]{:S(2)}) copy-start(bf16[2,1024,128]{2,1,0:T(8,128)(2,1)} %param.19) | copy-start | bytes 1572868
  132.7 21.6 %copy-start.3 = (f32[1024,128]{1,0:T(8,128)}, f32[1024,128]{1,0:T(8,128)S(1)}, u32[]{:S(2)}) copy-start(f32[1024,128]{1,0:T(8,128)S(1)} %get-tuple-element.48) | copy-start | bytes 1572868
  155.2 49.2 %copy-start.2 = (bf16[2,1024,128]{2,1,0:T(8,128)(2,1)S(1)}, bf16[2,1024,128]{2,1,0:T(8,128)(2,1)}, u32[]{:S(2)}) copy-start(bf16[2,1024,128]{2,1,0:T(8,128)(2,1)} %param.20) | copy-start | bytes 1572868
  155.5 49.1 %copy-start.7 = (bf16[2,2,128]{2,1,0:T(2,128)(2,1)S(1)}, bf16[2,2,128]{2,1,0:T(2,128)(2,1)}, u32[]{:S(2)}) copy-start(bf16[2,2,128]{2,1,0:T(2,128)(2,1)} %param.18) | copy-start | bytes 3076
Sparse Core Ops, SparseCore 0:
  12.3 91.0 reduce-scatter.1
  105.0 22.1 all-gather.5
  155.4 45.3 all-gather.3
